TPU v7x, 256 devices: a whole 4x4x8 slice. The times are simulated.
256 devices in a mesh: leaf: 256 (over x, z, y, core).
Axes of the slice: x: 4, y: 4, z: 8, core: 2. Of those that a mesh axis runs over, the one named last changes fastest.
Arguments:
- points: bfloat16 [64, 1048576], P(None, 'leaf'), may hold values from -5 to 5
- charges: bfloat16 [32, 1048576], P(None, 'leaf'), may hold values from -1.5 to 1.5
- leaf_order: int32 [256, 4096], P('leaf'), may hold values from 0 to 4095, each once within a row
- near_list: int32 [4096, 16], P('leaf'), may hold values from -1 to 4095, as said below
- far_list: int32 [2048, 8], P('leaf'), may hold values from -1 to 7
- local_skel: int32 [3840, 256], P('leaf'), may hold values from 0 to 511, as said below
- upper_skel: int32 [254, 256], replicated, may hold values from 0 to 511, as said below
Outputs:
- potentials: float32 [32, 1048576], P(None, 'leaf')
- root_field: float32 [256, 32, 256], P('leaf')
Inputs may be any that keep to these rules, and one draw needn't show every extreme that they name: `leaf_order`: each row is a permutation of the positions of one device's points. `near_list`: slot 0 of leaf g's row is g itself; every other entry is -1 or a leaf h different from g with |h - g| <= 16, and the leaves of one row are distinct. `far_list`: an entry other than -1 names a level-one node of the same device subtree, counted from that subtree's first level-one node; entries of a row may repeat. `local_skel`: the entries of a row are distinct. `upper_skel`: the entries of a row are distinct.
All inputs are finite; a program needn't handle non-finite values.
Results may differ from a plain program's by a relative error of at most 0.0014.
Values may be sent and summed in bfloat16 or wider, within the bound.
A program may use at most 64 MiB of HBM per device.

v0:
```python
import functools
import math

import jax
import jax.numpy as jnp
from jax import lax
from jax.experimental import pallas as pl
from jax.experimental.pallas import tpu as pltpu
from jax.sharding import PartitionSpec as P

f32 = jnp.float32
bf16 = jnp.bfloat16
MESH = pl.DeviceIdType.MESH
gain = math.sqrt(2.0)

LEFT, OWN, NODE, ZERO, RIGHT = 0, 16, 32, 47, 48


def dot(a, b):
    return jnp.dot(a, b, preferred_element_type=f32)


def dot_t(a, b):
    return lax.dot_general(a, b, (((1,), (1,)), ((), ())), preferred_element_type=f32)


def matern(scale, dist):
    positive = jnp.maximum(dist, 1e-30)
    radius = positive * lax.rsqrt(positive)
    return ((1.0 + radius * scale) * jnp.exp2(radius * (-scale * math.log2(math.e)))).astype(bf16)


def rows_of(block):
    columns = jnp.concatenate(
        [
            block[0:64].astype(f32) * -0.5,
            jnp.zeros((32, block.shape[1]), f32),
            block[112:128].astype(f32),
            block[96:112].astype(f32),
        ],
        axis=0,
    )
    return columns.T.astype(bf16)


def block_of(stacked):
    coords = stacked[0:64]
    square = jnp.sum(coords * coords, axis=0, keepdims=True)
    high = square.astype(bf16).astype(f32)
    rest = square - high
    middle = rest.astype(bf16).astype(f32)
    low = rest - middle
    place = lax.broadcasted_iota(jnp.int32, (16, stacked.shape[1]), 0)
    ones = jnp.where(place < 3, 1.0, 0.0)
    terms = jnp.where(place == 0, high, jnp.where(place == 1, middle, jnp.where(place == 2, low, 0.0)))
    return jnp.concatenate([coords * -2.0, stacked[64:96], ones, terms], axis=0).astype(bf16)


def one_hot(chosen, first, height=256):
    place = lax.broadcasted_iota(jnp.int32, (height, chosen.shape[1]), 0)
    return jnp.where(place == chosen - first, 1.0, 0.0).astype(bf16)


def lift(scale, left_block, right_block, left_rows, right_rows, chosen, kernel_ref):
    picked = dot(left_block, one_hot(chosen, 0)) + dot(right_block, one_hot(chosen, 256))
    target = picked.astype(bf16)
    first = matern(scale, dot(left_rows, target))
    second = matern(scale, dot(right_rows, target))
    kernel_ref[0] = first
    kernel_ref[1] = second
    sums = dot(left_block[64:112], first) + dot(right_block[64:112], second)
    weights = (gain * (sums[0:32] / sums[32:33])).astype(bf16)
    block = jnp.concatenate([target[0:64], weights, target[96:128]], axis=0)
    return block, rows_of(block)


def pushed(field, kernel):
    high = jnp.concatenate([field.astype(bf16), jnp.ones((16, field.shape[1]), bf16)], axis=0)
    sums = dot_t(high, kernel)
    return sums[0:32] / sums[32:33]


def sort_in(points, charges, order, source, blocks, rows):
    def fill(b, _):
        lanes = pl.ds(pl.multiple_of(b * 256, 256), 256)
        source[b, 0:64] = points[:, lanes]
        source[b, 64:96] = charges[:, lanes]
        return 0

    lax.fori_loop(0, 16, fill, 0)

    def leaf(g, _):
        ids = order[:, pl.ds(pl.multiple_of(g * 256, 256), 256)]
        found = dot(source[...].reshape(16 * 96, 256), one_hot(ids & 255, 0))
        high = ids >> 8
        stacked = found[0:96]
        for b in range(1, 16):
            stacked = jnp.where(high == b, found[b * 96 : b * 96 + 96], stacked)
        block = block_of(stacked)
        blocks[OWN + g] = block
        rows[OWN + g] = rows_of(block)
        return 0

    lax.fori_loop(0, 16, leaf, 0)


def sort_out(order, fields, output):
    output[...] = jnp.zeros_like(output)

    def leaf(g, _):
        ids = order[:, pl.ds(pl.multiple_of(g * 256, 256), 256)]
        picks = one_hot(ids & 255, 0)
        high = ids >> 8
        value = fields[g]
        first = value.astype(bf16).astype(f32)
        rest = value - first
        second = rest.astype(bf16).astype(f32)
        third = rest - second
        terms = jnp.concatenate([first, second, third], axis=0)
        for part in range(4):
            masked = jnp.concatenate(
                [jnp.where(high == part * 4 + b, terms, 0.0).astype(bf16) for b in range(4)], axis=0
            )
            found = dot_t(masked, picks)
            for b in range(4):
                lanes = slice((part * 4 + b) * 256, (part * 4 + b + 1) * 256)
                piece = found[b * 96 : b * 96 + 96]
                output[:, lanes] += piece[0:32] + piece[32:64] + piece[64:96]
        return 0

    lax.fori_loop(0, 16, leaf, 0)


def local_up(scale, skel, blocks, rows, kernels):
    def one(n):
        a, b = OWN + 2 * n, OWN + 1 + 2 * n
        block, flat = lift(
            scale, blocks[a], blocks[b], rows[a], rows[b], skel[pl.ds(n, 1), :], kernels.at[n]
        )
        blocks[NODE + n] = block
        rows[NODE + n] = flat

    def two(p, _):
        one(2 * p)
        one(2 * p + 1)
        return 0

    lax.fori_loop(0, 7, two, 0)
    one(14)


def local_down(fields, kernels):
    def one(n):
        field = fields[16 + n]
        fields[2 * n] += pushed(field, kernels[n, 0])
        fields[2 * n + 1] += pushed(field, kernels[n, 1])

    one(14)

    def two(p, _):
        one(13 - 2 * p)
        one(12 - 2 * p)
        return 0

    lax.fori_loop(0, 7, two, 0)


def couple_pair(scale, blocks, rows, fields, a, b):
    kernel = matern(scale, dot(rows[NODE + a], blocks[NODE + b]))
    fields[16 + b] = dot(blocks[NODE + a, 64:96], kernel)
    fields[16 + a] = dot_t(blocks[NODE + b, 64:96], kernel)


def far_counts(far_list):
    def count(i, b):
        total = jnp.where(b == i + 1 - 2 * (i % 2), 1.0, 0.0)
        for e in range(8):
            total = total + jnp.where(far_list[i, e] == b, 1.0, 0.0)
        return total

    return count


def far_own(scale, count, blocks, rows, fields):
    def own(i, _):
        kernel = matern(scale, dot(rows[NODE + i], blocks[NODE + i]))
        fields[16 + i] = count(i, i) * dot(blocks[NODE + i, 64:96], kernel)
        return 0

    lax.fori_loop(0, 8, own, 0)


def far_pair(scale, count, blocks, rows, fields, i, b):
    kernel = matern(scale, dot(rows[NODE + b], blocks[NODE + i]))
    fields[16 + i] += count(i, b) * dot(blocks[NODE + b, 64:96], kernel)
    fields[16 + b] += count(b, i) * dot_t(blocks[NODE + i, 64:96], kernel)


def near_leaf(scale, me, near, blocks, rows, fields, g):
    target = blocks[OWN + g]
    total = jnp.zeros((32, 256), f32)
    for k in range(16):
        leaf = near[g, k]
        offset = jnp.clip(leaf - (me - 1) * 16, 0, 47)
        place = jnp.where(leaf < 0, ZERO, jnp.where(offset >= 32, offset + 16, offset))
        kernel = matern(scale, dot(rows[place], target))
        total = total + dot(blocks[place, 64:96], kernel)
    fields[g] = total


def kernel(
    scale,
    devices,
    points,
    charges,
    order,
    near,
    far_list,
    local_skel,
    upper_skel,
    potentials,
    root,
    blocks,
    rows,
    kernels,
    source,
    fields,
    chain,
    chain_rows,
    chain_kernels,
    chain_fields,
    side_sent,
    side_got,
    up_sent,
    up_got,
):
    me = lax.axis_index("leaf")
    levels = devices.bit_length() - 1
    after, before = (me + 1) % devices, (me + devices - 1) % devices

    def bit_of(power):
        return (me // power) % 2

    def partner_of(power):
        return me + power * (1 - 2 * bit_of(power))

    barrier = pltpu.get_barrier_semaphore()
    others = [after, before] + [partner_of(2**r) for r in range(levels)]
    for other in others:
        pl.semaphore_signal(barrier, inc=1, device_id=(other,), device_id_type=MESH)
    blocks[ZERO] = jnp.zeros((128, 256), bf16)
    rows[ZERO] = jnp.zeros((256, 128), bf16)
    sort_in(points, charges, order, source, blocks, rows)
    pl.semaphore_wait(barrier, len(others))

    def side_copy(side, target, other):
        return pltpu.make_async_remote_copy(
            src_ref=blocks.at[pl.ds(OWN, 16)],
            dst_ref=blocks.at[pl.ds(target, 16)],
            send_sem=side_sent.at[side],
            recv_sem=side_got.at[side],
            device_id=(other,),
            device_id_type=MESH,
        )

    sides = [side_copy(0, LEFT, after), side_copy(1, RIGHT, before)]
    for side in sides:
        side.start()
    local_up(scale, local_skel, blocks, rows, kernels)

    def up_copy(r, power):
        own = bit_of(power)
        return pltpu.make_async_remote_copy(
            src_ref=chain.at[r, own],
            dst_ref=chain.at[r, own],
            send_sem=up_sent.at[r],
            recv_sem=up_got.at[r],
            device_id=(partner_of(power),),
            device_id_type=MESH,
        )

    def place(r, power, block, flat):
        chain[r, bit_of(power)] = block
        chain_rows[r, bit_of(power)] = flat

    def meet(r, power, last):
        own = bit_of(power)
        up_copy(r, power).wait()
        chain_rows[r, 1 - own] = rows_of(chain[r, 1 - own])
        kernel = matern(scale, dot(chain_rows[r, 1 - own], chain[r, own]))
        chain_fields[r] = dot(chain[r, 1 - own, 64:96], kernel)
        if not last:
            row = devices - devices // power + me // (2 * power)
            block, flat = lift(
                scale,
                chain[r, 0],
                chain[r, 1],
                chain_rows[r, 0],
                chain_rows[r, 1],
                upper_skel[pl.ds(row, 1), :],
                chain_kernels.at[r],
            )
            place(r + 1, 2 * power, block, flat)
            up_copy(r + 1, 2 * power).start()

    count = far_counts(far_list)

    def pairs(lo, hi, steps):
        def body(i, _):
            for step in steps:
                far_pair(scale, count, blocks, rows, fields, i, (i + step) % 8)
            return 0

        lax.fori_loop(lo, hi, body, 0)

    def leaves(lo, size):
        def body(g, _):
            near_leaf(scale, me, near, blocks, rows, fields, g)
            return 0

        lax.fori_loop(lo, lo + size, body, 0)

    place(0, 1, blocks[NODE + 14], rows[NODE + 14])
    up_copy(0, 1).start()
    for a in (8, 10, 12):
        couple_pair(scale, blocks, rows, fields, a, a + 1)
    meet(0, 1, False)
    far_own(scale, count, blocks, rows, fields)
    meet(1, 2, False)
    pairs(0, 8, (1, 2, 3))
    meet(2, 4, False)
    pairs(0, 4, (4,))
    for side in sides:
        side.wait()

    def side_rows(g, _):
        rows[LEFT + g] = rows_of(blocks[LEFT + g])
        rows[RIGHT + g] = rows_of(blocks[RIGHT + g])
        return 0

    lax.fori_loop(0, 16, side_rows, 0)

    def step(t, power):
        leaves(4 * t, 4)
        meet(t + 3, power, False)
        return 2 * power

    lax.fori_loop(0, 4, step, 8)
    meet(7, 128, True)
    for r in range(levels - 2, -1, -1):
        chain_fields[r] += pushed(chain_fields[r + 1], chain_kernels[r, bit_of(2**r)])
    root[0] = chain_fields[0]
    fields[30] = chain_fields[0]
    local_down(fields, kernels)
    sort_out(order, fields, potentials)


def solution(mesh):
    devices = mesh.shape["leaf"]

    def local(points, charges, order, near, far_list, local_skel, upper_skel):
        vmem = pl.BlockSpec(memory_space=pltpu.VMEM)
        smem = pl.BlockSpec(memory_space=pltpu.SMEM)
        return pl.pallas_call(
            functools.partial(kernel, 2.0 * math.sqrt(3.0 / 64), devices),
            out_shape=(
                jax.ShapeDtypeStruct((32, 4096), f32),
                jax.ShapeDtypeStruct((1, 32, 256), f32),
            ),
            in_specs=[vmem, vmem, vmem, smem, smem, vmem, vmem],
            out_specs=(vmem, vmem),
            scratch_shapes=[
                pltpu.VMEM((64, 128, 256), bf16),
                pltpu.VMEM((64, 256, 128), bf16),
                pltpu.VMEM((15, 2, 256, 256), bf16),
                pltpu.VMEM((16, 96, 256), bf16),
                pltpu.VMEM((31, 32, 256), f32),
                pltpu.VMEM((8, 2, 128, 256), bf16),
                pltpu.VMEM((8, 2, 256, 128), bf16),
                pltpu.VMEM((7, 2, 256, 256), bf16),
                pltpu.VMEM((8, 32, 256), f32),
                pltpu.SemaphoreType.DMA((2,)),
                pltpu.SemaphoreType.DMA((2,)),
                pltpu.SemaphoreType.DMA((8,)),
                pltpu.SemaphoreType.DMA((8,)),
            ],
            compiler_params=pltpu.CompilerParams(
                collective_id=0, has_side_effects=True, vmem_limit_bytes=60 << 20
            ),
            name="tree",
        )(points, charges, order, near, far_list, local_skel, upper_skel)

    placed = (
        P(None, "leaf"),
        P(None, "leaf"),
        P("leaf", None),
        P("leaf", None),
        P("leaf", None),
        P("leaf", None),
        P(),
    )
    return jax.shard_map(
        local,
        mesh=mesh,
        in_specs=placed,
        out_specs=(P(None, "leaf"), P("leaf", None, None)),
        check_vma=False,
    )
```

profile of v0, /device:TPU:1, one launch (start us, length us, event | category | flops | bytes accessed | tf_op | source)
XLA Modules:
  0.0 95.5 jit_solution(7195000847785119679)
XLA Ops:
  0.6 92.4 %tree.1 = (f32[32,4096]{1,0:T(8,128)}, f32[1,32,256]{2,1,0:T(8,128)}) custom-call(bf16[64,4096]{1,0:T(8,128)(2,1)} %points.1, bf16[32,4096]{1,0:T(8,128)(2,1)} %charges.1, s32[1,4096]{1,0:T(1,128)} %order.1, s32[16,16]{1,0:T(8,128)} %near.1, s32[8,8]{1,0:T(8,128)} %far_list.1, s32[15,256]{1,0:T(8,128)} %local_skel.1, s32[254,256]{1,0:T(8,128)} %upper_skel.1), custom_call_target="tpu_custom_call" | custom-call | tf_op jit(solution)/shard_map/tree/pallas_call | solution.py:364
  93.0 0.0 copy-start
  93.0 1.9 %copy.11 = f32[32,4096]{1,0:T(8,128)} copy(f32[32,4096]{1,0:T(8,128)} %get-tuple-element.4) | data formatting | bytes 1048576
  94.9 0.0 copy-done
  94.9 0.6 copy.12
Async XLA Ops:
  93.0 1.9 %copy-start = (f32[1,32,256]{2,1,0:T(8,128)S(1)}, f32[1,32,256]{2,1,0:T(8,128)}, u32[]{:S(2)}) copy-start(f32[1,32,256]{2,1,0:T(8,128)} %get-tuple-element.5) | copy-start | bytes 98308
where the time goes:
time: 95.7 us; the launch traced here: 95.5 us
  Pallas kernels  92.4 us (97%)
  local copies, waits for them, and re-layouts  2.49 us (3%)
    pallas_call x1, Pallas kernels, local(): pl.pallas_call(functools.partial(kernel, 2.0 * math.sqrt(3.0 / 64), devic...  92.4 us
    unnamed x4, local copies, waits for them, and re-layouts  2.49 us

commit v1 on v0

v1 whole, which is shorter than its diff:
```python
import functools
import math

import jax
import jax.numpy as jnp
from jax import lax
from jax.experimental import pallas as pl
from jax.experimental.pallas import tpu as pltpu
from jax.sharding import PartitionSpec as P

f32 = jnp.float32
bf16 = jnp.bfloat16
MESH = pl.DeviceIdType.MESH
gain = math.sqrt(2.0)

LEFT, OWN, NODE, ZERO, RIGHT = 0, 16, 32, 47, 48


def dot(a, b):
    return jnp.dot(a, b, preferred_element_type=f32)


def dot_t(a, b):
    return lax.dot_general(a, b, (((1,), (1,)), ((), ())), preferred_element_type=f32)


def matern(scale, dist):
    positive = jnp.maximum(dist, 1e-30)
    radius = positive * lax.rsqrt(positive)
    return ((1.0 + radius * scale) * jnp.exp2(radius * (-scale * math.log2(math.e)))).astype(bf16)


def rows_of(block):
    columns = jnp.concatenate(
        [block[0:64] * -0.5, jnp.zeros((32, block.shape[1]), bf16), block[112:128], block[96:112]], axis=0
    )
    return columns.T


def block_of(stacked):
    coords = stacked[0:64]
    square = jnp.sum(coords * coords, axis=0, keepdims=True)
    high = square.astype(bf16).astype(f32)
    rest = square - high
    middle = rest.astype(bf16).astype(f32)
    low = rest - middle
    place = lax.broadcasted_iota(jnp.int32, (16, stacked.shape[1]), 0)
    ones = jnp.where(place < 3, 1.0, 0.0)
    terms = jnp.where(place == 0, high, jnp.where(place == 1, middle, jnp.where(place == 2, low, 0.0)))
    return jnp.concatenate([coords * -2.0, stacked[64:96], ones, terms], axis=0).astype(bf16)


def one_hot(chosen, first, height=256):
    place = lax.broadcasted_iota(jnp.int32, (height, chosen.shape[1]), 0)
    return jnp.where(place == chosen - first, 1.0, 0.0).astype(bf16)


def stream(scale, stage, jobs):
    for k in range(len(jobs) + 1):
        if k < len(jobs):
            source, target = jobs[k][0](), jobs[k][1]()
            for c in (0, 128):
                stage[k % 2, c : c + 128] = matern(scale, dot(source[c : c + 128], target))
        if k > 0:
            jobs[k - 1][2](stage.at[(k - 1) % 2])


def lift_many(scale, nodes):
    targets = []
    for left, right, _, _, chosen, _, out, out_rows in nodes:
        picked = dot(left[...], one_hot(chosen, 0)) + dot(right[...], one_hot(chosen, 256))
        target = picked.astype(bf16)
        targets.append(target)
        out[...] = target
        out_rows[...] = rows_of(target)
    halves = [(i, h) for i in range(len(nodes)) for h in range(2)]
    sums = [None] * len(nodes)

    def use(i, h):
        part = dot(nodes[i][h][64:112], nodes[i][5][h])
        sums[i] = part if h == 0 else sums[i] + part
        if h == 1:
            nodes[i][6][64:96] = (gain * (sums[i][0:32] / sums[i][32:33])).astype(bf16)

    for k, (i, h) in enumerate(halves):
        source = nodes[i][2 + h]
        for c in (0, 128):
            nodes[i][5][h, c : c + 128] = matern(scale, dot(source[c : c + 128], targets[i]))
        if k > 0:
            use(*halves[k - 1])
    use(*halves[-1])


def pushed(field, kernel):
    high = jnp.concatenate([field.astype(bf16), jnp.ones((16, field.shape[1]), bf16)], axis=0)
    sums = dot_t(high, kernel)
    return sums[0:32] / sums[32:33]


def sort_in(points, charges, order, source, blocks, rows):
    def fill(b, _):
        lanes = pl.ds(pl.multiple_of(b * 256, 256), 256)
        source[b, 0:64] = points[:, lanes]
        source[b, 64:96] = charges[:, lanes]
        return 0

    lax.fori_loop(0, 16, fill, 0)

    def leaf(g):
        ids = order[:, pl.ds(pl.multiple_of(g * 256, 256), 256)]
        picks = one_hot(ids & 255, 0)
        high = ids >> 8
        stacked = None
        for part in range(SPLIT_IN):
            size = 16 // SPLIT_IN
            found = dot(source[part * size : part * size + size].reshape(size * 96, 256), picks)
            for b in range(size):
                piece = found[b * 96 : b * 96 + 96]
                stacked = piece if stacked is None else jnp.where(high == part * size + b, piece, stacked)
        block = block_of(stacked)
        blocks[OWN + g] = block
        rows[OWN + g] = rows_of(block)

    def some(p, _):
        for q in range(UNROLL_IN):
            leaf(UNROLL_IN * p + q)
        return 0

    lax.fori_loop(0, 16 // UNROLL_IN, some, 0)


SPLIT_IN = 4
UNROLL_IN = 4
UNROLL_OUT = 4
PARTS_OUT = 4
UP_BATCHES = ((0, 1, 2, 3), (4, 5, 6, 7), (8, 9, 10, 11), (12, 13), (14,))


def sort_out(order, fields, output):
    output[...] = jnp.zeros_like(output)

    def some(p, _):
        highs, picks, terms = [], [], []
        for q in range(UNROLL_OUT):
            g = UNROLL_OUT * p + q
            ids = order[:, pl.ds(pl.multiple_of(g * 256, 256), 256)]
            hot = one_hot(ids & 255, 0)
            value = fields[g]
            first = value.astype(bf16)
            second = (value - first.astype(f32)).astype(bf16)
            highs += [ids >> 8]
            picks += [hot, hot]
            terms += [[first, second]]
        picks = jnp.concatenate(picks, axis=1)
        size = 16 // PARTS_OUT
        for part in range(PARTS_OUT):
            masked = []
            for b in range(part * size, part * size + size):
                row = []
                for q in range(UNROLL_OUT):
                    mask = jnp.where(highs[q] == b, 1.0, 0.0).astype(bf16)
                    row += [terms[q][0] * mask, terms[q][1] * mask]
                masked.append(jnp.concatenate(row, axis=1))
            found = dot_t(jnp.concatenate(masked, axis=0), picks)
            for b in range(size):
                lanes = slice((part * size + b) * 256, (part * size + b + 1) * 256)
                output[:, lanes] += found[b * 32 : b * 32 + 32]
        return 0

    lax.fori_loop(0, 16 // UNROLL_OUT, some, 0)


def local_up(scale, skel, blocks, rows, kernels):
    for batch in UP_BATCHES:
        lift_many(
            scale,
            [
                (
                    blocks.at[OWN + 2 * n],
                    blocks.at[OWN + 1 + 2 * n],
                    rows.at[OWN + 2 * n],
                    rows.at[OWN + 1 + 2 * n],
                    skel[n : n + 1, :],
                    kernels.at[n],
                    blocks.at[NODE + n],
                    rows.at[NODE + n],
                )
                for n in batch
            ],
        )


def local_down(fields, kernels):
    def one(n):
        field = fields[16 + n]
        fields[2 * n] += pushed(field, kernels[n, 0])
        fields[2 * n + 1] += pushed(field, kernels[n, 1])

    one(14)

    def two(p, _):
        one(13 - 2 * p)
        one(12 - 2 * p)
        return 0

    lax.fori_loop(0, 7, two, 0)


def far(scale, far_list, blocks, rows, fields, stage, pairs):
    def count(i, b):
        total = 1.0 if b == i ^ 1 else 0.0
        for e in range(8):
            total = total + jnp.where(far_list[i, e] == b, 1.0, 0.0)
        return total

    def use(i, b, kernel):
        fields[16 + i] += count(i, b) * dot(blocks[NODE + b, 64:96], kernel[...])
        if i != b:
            fields[16 + b] += count(b, i) * dot_t(blocks[NODE + i, 64:96], kernel[...])

    jobs = [
        (
            functools.partial(lambda b: rows[NODE + b], b),
            functools.partial(lambda i: blocks[NODE + i], i),
            functools.partial(use, i, b),
        )
        for i, b in pairs
    ]
    stream(scale, stage, jobs)


def couple(scale, blocks, rows, fields, stage, pairs):
    def use(a, b, kernel):
        fields[16 + b] = dot(blocks[NODE + a, 64:96], kernel[...])
        fields[16 + a] = dot_t(blocks[NODE + b, 64:96], kernel[...])

    jobs = [
        (
            functools.partial(lambda a: rows[NODE + a], a),
            functools.partial(lambda b: blocks[NODE + b], b),
            functools.partial(use, a, b),
        )
        for a, b in pairs
    ]
    stream(scale, stage, jobs)


FAR_PAIRS = [(i, i) for i in range(8)] + [(i, i ^ d) for d in range(1, 8) for i in range(8) if i < i ^ d]


def near_steps(scale, me, near, blocks, rows, fields, stage, g):
    target = blocks[OWN + g]
    total = [jnp.zeros((32, 256), f32)]

    def place(k):
        leaf = near[g, k]
        offset = jnp.clip(leaf - (me - 1) * 16, 0, 47)
        return jnp.where(leaf < 0, ZERO, jnp.where(offset >= 32, offset + 16, offset))

    places = [place(k) for k in range(16)]

    def one(k):
        if k < 16:
            for c in (0, 128):
                stage[k % 2, c : c + 128] = matern(scale, dot(rows[places[k], c : c + 128], target))
        if k > 0:
            total[0] = total[0] + dot(blocks[places[k - 1], 64:96], stage[(k - 1) % 2])
        if k == 16:
            fields[g] = total[0]

    return [functools.partial(one, k) for k in range(17)]


def run(steps, others=(), every=2):
    others = list(others)
    for k, step in enumerate(steps):
        step()
        if others and k % every == 0:
            others.pop(0)()
    for other in others:
        other()


def kernel(
    scale,
    devices,
    points,
    charges,
    order,
    near,
    far_list,
    local_skel,
    upper_skel,
    potentials,
    root,
    blocks,
    rows,
    kernels,
    source,
    fields,
    chain,
    chain_rows,
    chain_kernels,
    chain_fields,
    stage,
    chain_stage,
    side_sent,
    side_got,
    up_sent,
    up_got,
):
    me = lax.axis_index("leaf")
    levels = devices.bit_length() - 1
    after, before = (me + 1) % devices, (me + devices - 1) % devices

    def bit_of(power):
        return (me // power) % 2

    def partner_of(power):
        return me + power * (1 - 2 * bit_of(power))

    barrier = pltpu.get_barrier_semaphore()
    others = [after, before] + [partner_of(2**r) for r in range(levels)]
    for other in others:
        pl.semaphore_signal(barrier, inc=1, device_id=(other,), device_id_type=MESH)
    blocks[ZERO] = jnp.zeros((128, 256), bf16)
    rows[ZERO] = jnp.zeros((256, 128), bf16)
    sort_in(points, charges, order, source, blocks, rows)
    pl.semaphore_wait(barrier, len(others))

    def side_copy(side, target, other):
        return pltpu.make_async_remote_copy(
            src_ref=blocks.at[pl.ds(OWN, 16)],
            dst_ref=blocks.at[pl.ds(target, 16)],
            send_sem=side_sent.at[side],
            recv_sem=side_got.at[side],
            device_id=(other,),
            device_id_type=MESH,
        )

    sides = [side_copy(0, LEFT, after), side_copy(1, RIGHT, before)]
    for side in sides:
        side.start()
    local_up(scale, local_skel, blocks, rows, kernels)

    def up_copy(r, power):
        own = bit_of(power)
        return pltpu.make_async_remote_copy(
            src_ref=chain.at[r, own],
            dst_ref=chain.at[r, own],
            send_sem=up_sent.at[r],
            recv_sem=up_got.at[r],
            device_id=(partner_of(power),),
            device_id_type=MESH,
        )

    def place(r, power, block, flat):
        chain[r, bit_of(power)] = block
        chain_rows[r, bit_of(power)] = flat

    def meet_steps(r, power, last):
        own = bit_of(power)
        kept = {}

        def sibling():
            chain_rows[r, 1 - own] = rows_of(chain[r, 1 - own])

        def pick():
            row = devices - devices // power + me // (2 * power)
            chosen = upper_skel[pl.ds(row, 1), :]
            picked = dot(chain[r, 0], one_hot(chosen, 0)) + dot(chain[r, 1], one_hot(chosen, 256))
            kept["target"] = picked.astype(bf16)

        def flat():
            chain_rows[r + 1, bit_of(2 * power)] = rows_of(kept["target"])

        def half(h):
            for c in (0, 128):
                piece = matern(scale, dot(chain_rows[r, h, c : c + 128], kept["target"]))
                chain_kernels[r, h, c : c + 128] = piece

        def weigh():
            sums = dot(chain[r, 0, 64:112], chain_kernels[r, 0])
            sums = sums + dot(chain[r, 1, 64:112], chain_kernels[r, 1])
            weights = (gain * (sums[0:32] / sums[32:33])).astype(bf16)
            target = kept["target"]
            chain[r + 1, bit_of(2 * power)] = jnp.concatenate(
                [target[0:64], weights, target[96:128]], axis=0
            )

        def couple_kernel():
            for c in (0, 128):
                chain_stage[c : c + 128] = matern(
                    scale, dot(chain_rows[r, 1 - own, c : c + 128], chain[r, own])
                )

        def couple_use():
            chain_fields[r] = dot(chain[r, 1 - own, 64:96], chain_stage[...])

        if last:
            return [sibling, couple_kernel, couple_use]
        return [
            sibling,
            pick,
            functools.partial(half, 0),
            functools.partial(half, 1),
            weigh,
            flat,
            couple_kernel,
            couple_use,
        ]

    def down(r):
        chain_fields[r] += pushed(chain_fields[r + 1], chain_kernels[r, bit_of(2**r)])

    def leaf(g):
        return near_steps(scale, me, near, blocks, rows, fields, stage, g)

    chain[0, bit_of(1)] = blocks[NODE + 14]
    chain_rows[0, bit_of(1)] = rows[NODE + 14]
    up_copy(0, 1).start()
    fields[16:24] = jnp.zeros((8, 32, 256), f32)
    couple(scale, blocks, rows, fields, stage, [(8, 9), (10, 11), (12, 13)])
    far(scale, far_list, blocks, rows, fields, stage, FAR_PAIRS)
    for side in sides:
        side.wait()

    def side_rows(g, _):
        rows[LEFT + g] = rows_of(blocks[LEFT + g])
        rows[RIGHT + g] = rows_of(blocks[RIGHT + g])
        return 0

    lax.fori_loop(0, 16, side_rows, 0)

    def step(r, power):
        run(leaf(2 * r))
        up_copy(r, power).wait()
        run(leaf(2 * r + 1), meet_steps(r, power, False))
        up_copy(r + 1, 2 * power).start()
        return 2 * power

    lax.fori_loop(0, levels - 1, step, 1)
    run(leaf(14))
    up_copy(levels - 1, devices // 2).wait()
    downs = [functools.partial(down, r) for r in range(levels - 2, -1, -1)]
    run(leaf(15), meet_steps(levels - 1, devices // 2, True) + downs, every=1)
    root[0] = chain_fields[0]
    fields[30] = chain_fields[0]
    local_down(fields, kernels)
    sort_out(order, fields, potentials)


def solution(mesh):
    devices = mesh.shape["leaf"]

    def local(points, charges, order, near, far_list, local_skel, upper_skel):
        vmem = pl.BlockSpec(memory_space=pltpu.VMEM)
        smem = pl.BlockSpec(memory_space=pltpu.SMEM)
        return pl.pallas_call(
            functools.partial(kernel, 2.0 * math.sqrt(3.0 / 64), devices),
            out_shape=(
                jax.ShapeDtypeStruct((32, 4096), f32),
                jax.ShapeDtypeStruct((1, 32, 256), f32),
            ),
            in_specs=[vmem, vmem, vmem, smem, smem, vmem, vmem],
            out_specs=(vmem, vmem),
            scratch_shapes=[
                pltpu.VMEM((64, 128, 256), bf16),
                pltpu.VMEM((64, 256, 128), bf16),
                pltpu.VMEM((15, 2, 256, 256), bf16),
                pltpu.VMEM((16, 96, 256), bf16),
                pltpu.VMEM((31, 32, 256), f32),
                pltpu.VMEM((8, 2, 128, 256), bf16),
                pltpu.VMEM((8, 2, 256, 128), bf16),
                pltpu.VMEM((7, 2, 256, 256), bf16),
                pltpu.VMEM((8, 32, 256), f32),
                pltpu.VMEM((2, 256, 256), bf16),
                pltpu.VMEM((256, 256), bf16),
                pltpu.SemaphoreType.DMA((2,)),
                pltpu.SemaphoreType.DMA((2,)),
                pltpu.SemaphoreType.DMA((8,)),
                pltpu.SemaphoreType.DMA((8,)),
            ],
            compiler_params=pltpu.CompilerParams(
                collective_id=0, has_side_effects=True, vmem_limit_bytes=60 << 20
            ),
            name="tree",
        )(points, charges, order, near, far_list, local_skel, upper_skel)

    placed = (
        P(None, "leaf"),
        P(None, "leaf"),
        P("leaf", None),
        P("leaf", None),
        P("leaf", None),
        P("leaf", None),
        P(),
    )
    return jax.shard_map(
        local,
        mesh=mesh,
        in_specs=placed,
        out_specs=(P(None, "leaf"), P("leaf", None, None)),
        check_vma=False,
    )
```

time: 95.7 us -> 88.7 us (0.927)
  the two profiles are of different devices: /device:TPU:1 before, /device:TPU:24 now
where the time goes in v1:
time: 88.7 us; the launch traced here: 88.6 us
  Pallas kernels  85.4 us (96%)
  local copies, waits for them, and re-layouts  2.49 us (3%)
    pallas_call x1, Pallas kernels, local(): pl.pallas_call(functools.partial(kernel, 2.0 * math.sqrt(3.0 / 64), devic...  85.4 us
    unnamed x4, local copies, waits for them, and re-layouts  2.49 us

profile of v1, /device:TPU:24, one launch (start us, length us, event | category | flops | bytes accessed | tf_op | source)
XLA Modules:
  0.0 88.6 jit_solution(4376618601591232961)
XLA Ops:
  0.6 85.4 %tree.1 = (f32[32,4096]{1,0:T(8,128)}, f32[1,32,256]{2,1,0:T(8,128)}) custom-call(bf16[64,4096]{1,0:T(8,128)(2,1)} %points.1, bf16[32,4096]{1,0:T(8,128)(2,1)} %charges.1, s32[1,4096]{1,0:T(1,128)} %order.1, s32[16,16]{1,0:T(8,128)} %near.1, s32[8,8]{1,0:T(8,128)} %far_list.1, s32[15,256]{1,0:T(8,128)} %local_skel.1, s32[254,256]{1,0:T(8,128)} %upper_skel.1), custom_call_target="tpu_custom_call" | custom-call | tf_op jit(solution)/shard_map/tree/pallas_call | solution.py:459
  86.1 0.0 copy-start
  86.1 1.9 %copy.11 = f32[32,4096]{1,0:T(8,128)} copy(f32[32,4096]{1,0:T(8,128)} %get-tuple-element.4) | data formatting | bytes 1048576
  87.9 0.0 copy-done
  87.9 0.6 copy.12
Async XLA Ops:
  86.1 1.9 %copy-start = (f32[1,32,256]{2,1,0:T(8,128)S(1)}, f32[1,32,256]{2,1,0:T(8,128)}, u32[]{:S(2)}) copy-start(f32[1,32,256]{2,1,0:T(8,128)} %get-tuple-element.5) | copy-start | bytes 98308

commit v2 on v1

--- a/solution.py
+++ b/solution.py
@@ -37,17 +37,27 @@
     return columns.T
 
 
-def block_of(stacked):
-    coords = stacked[0:64]
+def tail_of(coords):
     square = jnp.sum(coords * coords, axis=0, keepdims=True)
     high = square.astype(bf16).astype(f32)
     rest = square - high
     middle = rest.astype(bf16).astype(f32)
     low = rest - middle
-    place = lax.broadcasted_iota(jnp.int32, (16, stacked.shape[1]), 0)
+    place = lax.broadcasted_iota(jnp.int32, (16, coords.shape[1]), 0)
     ones = jnp.where(place < 3, 1.0, 0.0)
     terms = jnp.where(place == 0, high, jnp.where(place == 1, middle, jnp.where(place == 2, low, 0.0)))
-    return jnp.concatenate([coords * -2.0, stacked[64:96], ones, terms], axis=0).astype(bf16)
+    return jnp.concatenate([ones, terms], axis=0).astype(bf16)
+
+
+def block_of(stacked):
+    coords = stacked[0:64]
+    whole = jnp.concatenate([coords * -2.0, stacked[64:96]], axis=0).astype(bf16)
+    return jnp.concatenate([whole, tail_of(coords)], axis=0)
+
+
+def complete(block, rows):
+    block[96:128] = tail_of(block[0:64].astype(f32) * -0.5)
+    rows[...] = rows_of(block[...])
 
 
 def one_hot(chosen, first, height=256):
@@ -330,8 +340,8 @@
 
     def side_copy(side, target, other):
         return pltpu.make_async_remote_copy(
-            src_ref=blocks.at[pl.ds(OWN, 16)],
-            dst_ref=blocks.at[pl.ds(target, 16)],
+            src_ref=blocks.at[pl.ds(OWN, 16), 0:96],
+            dst_ref=blocks.at[pl.ds(target, 16), 0:96],
             send_sem=side_sent.at[side],
             recv_sem=side_got.at[side],
             device_id=(other,),
@@ -346,8 +356,8 @@
     def up_copy(r, power):
         own = bit_of(power)
         return pltpu.make_async_remote_copy(
-            src_ref=chain.at[r, own],
-            dst_ref=chain.at[r, own],
+            src_ref=chain.at[r, own, 0:96],
+            dst_ref=chain.at[r, own, 0:96],
             send_sem=up_sent.at[r],
             recv_sem=up_got.at[r],
             device_id=(partner_of(power),),
@@ -363,7 +373,7 @@
         kept = {}
 
         def sibling():
-            chain_rows[r, 1 - own] = rows_of(chain[r, 1 - own])
+            complete(chain.at[r, 1 - own], chain_rows.at[r, 1 - own])
 
         def pick():
             row = devices - devices // power + me // (2 * power)
@@ -404,9 +414,9 @@
             pick,
             functools.partial(half, 0),
             functools.partial(half, 1),
+            couple_kernel,
             weigh,
             flat,
-            couple_kernel,
             couple_use,
         ]
 
@@ -419,28 +429,39 @@
     chain[0, bit_of(1)] = blocks[NODE + 14]
     chain_rows[0, bit_of(1)] = rows[NODE + 14]
     up_copy(0, 1).start()
+    def meet(r, power):
+        up_copy(r, power).wait()
+        run(meet_steps(r, power, False))
+        up_copy(r + 1, 2 * power).start()
+
     fields[16:24] = jnp.zeros((8, 32, 256), f32)
     couple(scale, blocks, rows, fields, stage, [(8, 9), (10, 11), (12, 13)])
+    meet(0, 1)
     far(scale, far_list, blocks, rows, fields, stage, FAR_PAIRS)
+    meet(1, 2)
     for side in sides:
         side.wait()
 
     def side_rows(g, _):
-        rows[LEFT + g] = rows_of(blocks[LEFT + g])
-        rows[RIGHT + g] = rows_of(blocks[RIGHT + g])
+        complete(blocks.at[LEFT + g], rows.at[LEFT + g])
+        complete(blocks.at[RIGHT + g], rows.at[RIGHT + g])
         return 0
 
     lax.fori_loop(0, 16, side_rows, 0)
 
+    def some(g, _):
+        run(leaf(g))
+        return 0
+
     def step(r, power):
-        run(leaf(2 * r))
-        up_copy(r, power).wait()
-        run(leaf(2 * r + 1), meet_steps(r, power, False))
-        up_copy(r + 1, 2 * power).start()
+        lo = jnp.where(r < 3, 0, jnp.where(r < 4, 1, jnp.where(r < 5, 3, jnp.where(r < 6, 6, 11))))
+        hi = jnp.where(r < 3, 1, jnp.where(r < 4, 3, jnp.where(r < 5, 6, jnp.where(r < 6, 11, 13))))
+        lax.fori_loop(lo, hi, some, 0)
+        meet(r, power)
         return 2 * power
 
-    lax.fori_loop(0, levels - 1, step, 1)
-    run(leaf(14))
+    lax.fori_loop(2, levels - 1, step, 4)
+    lax.fori_loop(13, 15, some, 0)
     up_copy(levels - 1, devices // 2).wait()
     downs = [functools.partial(down, r) for r in range(levels - 2, -1, -1)]
     run(leaf(15), meet_steps(levels - 1, devices // 2, True) + downs, every=1)

time: 88.7 us -> 72.3 us (0.82)
  the two profiles are of different devices: /device:TPU:24 before, /device:TPU:1 now
where the time goes in v2:
time: 72.3 us; the launch traced here: 72.1 us
  Pallas kernels  69 us (95%)
  local copies, waits for them, and re-layouts  2.49 us (3%)
    pallas_call x1, Pallas kernels, local(): pl.pallas_call(functools.partial(kernel, 2.0 * math.sqrt(3.0 / 64), devic...  69 us
    unnamed x4, local copies, waits for them, and re-layouts  2.49 us

profile of v2, /device:TPU:1, one launch (start us, length us, event | category | flops | bytes accessed | tf_op | source)
XLA Modules:
  0.0 72.1 jit_solution(4625068369170326877)
XLA Ops:
  0.6 69.0 %tree.1 = (f32[32,4096]{1,0:T(8,128)}, f32[1,32,256]{2,1,0:T(8,128)}) custom-call(bf16[64,4096]{1,0:T(8,128)(2,1)} %points.1, bf16[32,4096]{1,0:T(8,128)(2,1)} %charges.1, s32[1,4096]{1,0:T(1,128)} %order.1, s32[16,16]{1,0:T(8,128)} %near.1, s32[8,8]{1,0:T(8,128)} %far_list.1, s32[15,256]{1,0:T(8,128)} %local_skel.1, s32[254,256]{1,0:T(8,128)} %upper_skel.1), custom_call_target="tpu_custom_call" | custom-call | tf_op jit(solution)/shard_map/tree/pallas_call | solution.py:480
  69.6 0.0 copy-start
  69.6 1.9 %copy.11 = f32[32,4096]{1,0:T(8,128)} copy(f32[32,4096]{1,0:T(8,128)} %get-tuple-element.4) | data formatting | bytes 1048576
  71.5 0.0 copy-done
  71.5 0.6 copy.12
Async XLA Ops:
  69.6 1.9 %copy-start = (f32[1,32,256]{2,1,0:T(8,128)S(1)}, f32[1,32,256]{2,1,0:T(8,128)}, u32[]{:S(2)}) copy-start(f32[1,32,256]{2,1,0:T(8,128)} %get-tuple-element.5) | copy-start | bytes 98308

commit v3 on v2

--- a/solution.py
+++ b/solution.py
@@ -141,8 +141,8 @@
 
 SPLIT_IN = 4
 UNROLL_IN = 4
-UNROLL_OUT = 4
-PARTS_OUT = 4
+UNROLL_OUT = 8
+PARTS_OUT = 2
 UP_BATCHES = ((0, 1, 2, 3), (4, 5, 6, 7), (8, 9, 10, 11), (12, 13), (14,))
 
 
@@ -201,19 +201,10 @@
 
 
 def local_down(fields, kernels):
-    def one(n):
+    for n in range(14, -1, -1):
         field = fields[16 + n]
         fields[2 * n] += pushed(field, kernels[n, 0])
         fields[2 * n + 1] += pushed(field, kernels[n, 1])
-
-    one(14)
-
-    def two(p, _):
-        one(13 - 2 * p)
-        one(12 - 2 * p)
-        return 0
-
-    lax.fori_loop(0, 7, two, 0)
 
 
 def far(scale, far_list, blocks, rows, fields, stage, pairs):
@@ -468,6 +459,11 @@
     root[0] = chain_fields[0]
     fields[30] = chain_fields[0]
     local_down(fields, kernels)
+    potentials[...] = fields[0:16]
+
+
+def finish(order, fields, root_in, potentials, root):
+    root[...] = root_in[...]
     sort_out(order, fields, potentials)
 
 
@@ -477,10 +473,10 @@
     def local(points, charges, order, near, far_list, local_skel, upper_skel):
         vmem = pl.BlockSpec(memory_space=pltpu.VMEM)
         smem = pl.BlockSpec(memory_space=pltpu.SMEM)
-        return pl.pallas_call(
+        fields, root = pl.pallas_call(
             functools.partial(kernel, 2.0 * math.sqrt(3.0 / 64), devices),
             out_shape=(
-                jax.ShapeDtypeStruct((32, 4096), f32),
+                jax.ShapeDtypeStruct((16, 32, 256), f32),
                 jax.ShapeDtypeStruct((1, 32, 256), f32),
             ),
             in_specs=[vmem, vmem, vmem, smem, smem, vmem, vmem],
@@ -507,6 +503,16 @@
             ),
             name="tree",
         )(points, charges, order, near, far_list, local_skel, upper_skel)
+        return pl.pallas_call(
+            finish,
+            out_shape=(
+                jax.ShapeDtypeStruct((32, 4096), f32),
+                jax.ShapeDtypeStruct((1, 32, 256), f32),
+            ),
+            in_specs=[vmem, vmem, vmem],
+            out_specs=(vmem, vmem),
+            name="finish",
+        )(order, fields, root)
 
     placed = (
         P(None, "leaf"),

time: 72.3 us -> 67 us (0.927)
  Pallas kernels: 69 us -> 66.2 us
  local copies, waits for them, and re-layouts: 2.49 us -> 0 us
    pallas_call x1, Pallas kernels: 69 us -> 61.7 us  [local(): pl.pallas_call(functools.partial(kernel, 2.0 * math.sqrt(3.0 / 64), devic...]
    pallas_call x0 -> x1, Pallas kernels: none -> 4.46 us  [local(): pl.pallas_call(finish, out_shape=(jax.ShapeDtypeStruct((32, 4096), f32),...]
    unnamed x4 -> x0, local copies, waits for them, and re-layouts: 2.49 us -> none
where the time goes in v3:
time: 67 us; the launch traced here: 66.8 us
  Pallas kernels  66.2 us (99%)
    pallas_call x1, Pallas kernels, local(): pl.pallas_call(functools.partial(kernel, 2.0 * math.sqrt(3.0 / 64), devic...  61.7 us
    pallas_call x1, Pallas kernels, local(): pl.pallas_call(finish, out_shape=(jax.ShapeDtypeStruct((32, 4096), f32),...  4.46 us

profile of v3, /device:TPU:1, one launch (start us, length us, event | category | flops | bytes accessed | tf_op | source)
XLA Modules:
  0.0 66.8 jit_solution(7067561817502352969)
XLA Ops:
  0.6 61.7 %tree.1 = (f32[16,32,256]{2,1,0:T(8,128)}, f32[1,32,256]{2,1,0:T(8,128)}) custom-call(bf16[64,4096]{1,0:T(8,128)(2,1)} %points.1, bf16[32,4096]{1,0:T(8,128)(2,1)} %charges.1, s32[1,4096]{1,0:T(1,128)} %order.3, s32[16,16]{1,0:T(8,128)} %near.1, s32[8,8]{1,0:T(8,128)} %far_list.1, s32[15,256]{1,0:T(8,128)} %local_skel.1, s32[254,256]{1,0:T(8,128)} %upper_skel.1), custom_call_target="tpu_custom_call" | custom-call | tf_op jit(solution)/shard_map/tree/pallas_call | solution.py:476
  62.3 4.5 %finish.1 = (f32[32,4096]{1,0:T(8,128)}, f32[1,32,256]{2,1,0:T(8,128)}) custom-call(s32[1,4096]{1,0:T(1,128)} %order.3, f32[16,32,256]{2,1,0:T(8,128)} %get-tuple-element.4.fields, f32[1,32,256]{2,1,0:T(8,128)} %get-tuple-element.5.root_in), custom_call_target="tpu_custom_call" | custom-call | tf_op jit(solution)/shard_map/finish/pallas_call | solution.py:506
